TPU v7x, 128 devices: a whole 4x4x4 slice. The times are simulated.
128 devices in a mesh: gz: 4 (over z), gy: 8 (over y, core), gx: 4 (over x).
Axes of the slice: x: 4, y: 4, z: 4, core: 2. Of those that a mesh axis runs over, the one named last changes fastest.
Arguments:
- ref_image: float32 [64, 512, 512], P('gz', 'gy', 'gx'), may hold values from -40 to 40
- deformed_image: float32 [64, 512, 512], P('gz', 'gy', 'gx'), may hold values from -40 to 40
- nodal_disp: int32 [3, 8, 40, 36], P(None, 'gz', 'gy', 'gx'), may hold values from -1024 to 1023, as said below
Outputs:
- update: float32 [3, 8, 40, 36], P(None, 'gz', 'gy', 'gx')
- cg_residual: float32 [3, 8, 40, 36], P(None, 'gz', 'gy', 'gx')
Inputs may be any that keep to these rules, and one draw needn't show every extreme that they name: `nodal_disp`: copies of a node held by neighbouring bricks are equal.
All inputs are finite; a program needn't handle non-finite values.
Results may differ from a plain program's by a relative error of at most 0.0003.
Values sent between devices are 32-bit elements; how exact they have to be, the bound alone decides.
No kernel may reach another device: no remote copies, remote signals or barrier semaphores. Data moves between devices by JAX's collectives and lax.ppermute only.
A program may use at most 256 MiB of HBM per device.

v0:
```python
import jax
import jax.numpy as jnp
import numpy as np
from jax import lax
from jax.experimental import pallas as pl
from jax.experimental.pallas import tpu as pltpu
from jax.sharding import PartitionSpec as P

E = 16
CGSTEPS = 8
QUANTUM = 64
DAMPING = 0.5
BZ, BY, BX = 16, 64, 128
NGZ, NGY, NGX = 4, 8, 4
JY, JX = 5, 9
BLK = JY * JX
HI = lax.Precision.HIGHEST
PAIRS = ((0, 0), (0, 1), (0, 2), (1, 1), (1, 2), (2, 2))
PAIR_OF = {(0, 0): 0, (0, 1): 1, (0, 2): 2, (1, 1): 3, (1, 2): 4, (2, 2): 5}
KROWS = 24
RROWS = 4
F32 = jnp.float32

_T = (np.arange(E) + 0.5) / E
_W0, _W1 = 1.0 - _T, _T


def _place(kinds, count):
    low, high, mixed = kinds
    rows = np.zeros((count + 1 + (count if mixed is not None else 0), count * E), np.float32)
    for e in range(count):
        rows[e, e * E:(e + 1) * E] += low
        rows[e + 1, e * E:(e + 1) * E] += high
        if mixed is not None:
            rows[count + 1 + e, e * E:(e + 1) * E] = mixed
    return rows


def _left(rows, fields):
    out = np.zeros((rows.shape[0] * 8, fields * BY), np.float32)
    for q in range(rows.shape[0]):
        for f in range(fields):
            out[q * 8 + f, f * BY:(f + 1) * BY] = rows[q]
    return out


def _right(rows, scale):
    out = np.zeros((BX, BX), np.float32)
    out[:, :rows.shape[0]] = rows.T * scale
    return out


_SQ = (_W0 * _W0, _W1 * _W1, _W0 * _W1)
_LIN = (_W0, _W1, None)
LEFT_K = _left(_place(_SQ, 4), 6)
RIGHT_K = _right(_place(_SQ, 8), 0.25 / E**2)
LEFT_R = _left(_place(_LIN, 4), 3)
RIGHT_R = _right(_place(_LIN, 8), 0.5 / E**2)


def lanes(shape=(8, BX)):
    return lax.broadcasted_iota(jnp.int32, shape, len(shape) - 1)


def roll(x, amount, axis=1):
    size = x.shape[axis]
    if isinstance(amount, int):
        amount %= size
        if amount == 0:
            return x
    return pltpu.roll(x, amount, axis)


VMEM = pl.BlockSpec(memory_space=pltpu.VMEM)
SMEM = pl.BlockSpec(memory_space=pltpu.SMEM)


def grant(mib):
    return pltpu.CompilerParams(vmem_limit_bytes=mib << 20)


PZ, PY = 3 * E, BY + 2 * E
GROUP = PZ // 8
STRIP = GROUP * PY + 8


def piece(blocks, z, tile):
    mid, zlo, zhi, ylo, yhi = blocks
    if tile < 2:
        return ylo[z, tile * 8:tile * 8 + 8, :]
    if tile >= 10:
        return yhi[z, (tile - 10) * 8:(tile - 10) * 8 + 8, :]
    return (zlo, mid, zhi)[z // E][z % E, (tile - 2) * 8:(tile - 2) * 8 + 8, :]


def columns(lane, g):
    return (lane >= 16 * g) & (lane < 16 * g + 16)


def strips_kernel(ref, mid, zlo, zhi, ylo, yhi, first, last):
    blocks = (mid, zlo, zhi, ylo, yhi)
    lane = lanes()
    for zz in range(GROUP):
        for tile in range(PY // 8):
            a = jnp.zeros((8, BX), F32)
            b = jnp.zeros((8, BX), F32)
            for g in range(8):
                v = piece(blocks, g * GROUP + zz, tile)
                v = roll(v, 16 * g)
                a = jnp.where(columns(lane, g), v, a)
                b = jnp.where(columns(lane, (g + 7) % 8), v, b)
            row = zz * PY + tile * 8
            first[row:row + 8, :] = a
            last[row:row + 8, :] = b
    a = jnp.zeros((8, BX), F32)
    b = jnp.zeros((8, BX), F32)
    for tile in range(BY // 8):
        for z in range(BZ):
            v = ref[z, tile * 8:tile * 8 + 8, :]
            to = 16 * tile + z
            a = jnp.where(lane == to, roll(v, to), a)
            b = jnp.where(lane == to, roll(v, to + 1), b)
    first[GROUP * PY:, :] = a
    last[GROUP * PY:, :] = b


def strips(ref, *blocks):
    shape = jax.ShapeDtypeStruct((STRIP, BX), F32)
    return pl.pallas_call(
        strips_kernel,
        out_shape=[shape, shape],
        in_specs=[VMEM] * 6,
        out_specs=[VMEM] * 2,
        compiler_params=grant(8),
        name="strips",
    )(ref, *blocks)


def warp_element(summed, tile, ey, ex, warped):
    lane = lanes((E, BX))
    e = ey * 8 + ex
    sz, sy, sx = summed[e], summed[32 + e], summed[64 + e]
    whole_z = lax.shift_right_arithmetic(sz, 9)
    whole_y = lax.shift_right_arithmetic(sy, 9)
    whole_x = lax.shift_right_arithmetic(sx, 9)
    scale = 1.0 / (8.0 * QUANTUM)
    fz = (sz & 511).astype(F32) * scale
    fy = (sy & 511).astype(F32) * scale
    fx = (sx & 511).astype(F32) * scale
    start_z = whole_z + E
    start_y = whole_y + E + ey * E
    turn = jnp.where(whole_x > 0, BX - whole_x, -whole_x)
    mask = (lane >= ex * 16) & (lane < ex * 16 + 16)
    row = pl.multiple_of(ey * E, E)

    def plane(k):
        a = tile[start_z + k, pl.ds(start_y, E), :]
        b = tile[start_z + k, pl.ds(start_y + 1, E), :]
        return (1.0 - fy) * a + fy * b

    below = plane(0)
    for k in range(E):
        above = plane(k + 1)
        v = (1.0 - fz) * below + fz * above
        v = pltpu.roll(v, turn, 1)
        v = (1.0 - fx) * v + fx * roll(v, BX - 1)
        pltpu.store(warped.at[k, pl.ds(row, E), :], v, mask=mask)
        below = above


def inner_kernel(summed, mid, zlo, zhi, ylo, yhi, warped, tile):
    blocks = (mid, zlo, zhi, ylo, yhi)
    for z in range(PZ):
        for t in range(PY // 8):
            tile[z, t * 8:t * 8 + 8, :] = piece(blocks, z, t)

    def pair(i, carry):
        for ex in range(2):
            warp_element(summed, tile, i // 3, 1 + 2 * (i % 3) + ex, warped)
        return carry

    lax.fori_loop(0, 12, pair, 0)


def inner(summed, *blocks):
    return pl.pallas_call(
        inner_kernel,
        out_shape=jax.ShapeDtypeStruct((BZ, BY, BX), F32),
        in_specs=[SMEM] + [VMEM] * 5,
        out_specs=VMEM,
        scratch_shapes=[pltpu.VMEM((PZ, PY, BX), F32)],
        compiler_params=grant(10),
        name="inner",
    )(summed, *blocks)


def slopes(pad, xlo, xhi, z, y, lane):
    here = pad[z + 1, pl.ds(8 + y, 8), :]
    along_z = pad[z + 2, pl.ds(8 + y, 8), :] - pad[z, pl.ds(8 + y, 8), :]
    along_y = pad[z + 1, pl.ds(9 + y, 8), :] - pad[z + 1, pl.ds(7 + y, 8), :]
    after_ = jnp.where(lane == BX - 1, roll(xhi, BX - 1 - z), roll(here, BX - 1))
    before = jnp.where(lane == 0, roll(xlo, -z), roll(here, 1))
    return (along_z, along_y, after_ - before), here


def terms_kernel(
    summed, ref, rzlo, rzhi, mid, zlo, zhi, ylo, yhi, xlo, xhi, inside,
    left_k, right_k, left_r, right_r, out, pad, tiles, warped, acc_k, acc_r,
):
    blocks = (mid, zlo, zhi, ylo, yhi)
    lane = lanes()
    pad[1:BZ + 1, 8:8 + BY, :] = ref[...]
    pad[0:1, 8:8 + BY, :] = rzlo[...]
    pad[BZ + 1:BZ + 2, 8:8 + BY, :] = rzhi[...]
    for z in range(BZ):
        pad[z + 1, 7:8, :] = ylo[PZ, z:z + 1, :]
        pad[z + 1, 8 + BY:9 + BY, :] = yhi[PZ, z:z + 1, :]
    for z in range(PZ):
        g, zz = z // GROUP, z % GROUP
        for t in range(PY // 8):
            v = piece(blocks, z, t)
            row = zz * PY + t * 8
            both = jnp.where(columns(lane, (g + 7) % 8), xlo[row:row + 8, :], xhi[row:row + 8, :])
            both = roll(both, -16 * g)
            tiles[0, z, t * 8:t * 8 + 8, :] = jnp.where(lane >= 112, both, v)
            tiles[1, z, t * 8:t * 8 + 8, :] = jnp.where(lane < 16, both, v)

    def element(ey, carry):
        warp_element(summed, tiles.at[0], ey, 0, warped)
        warp_element(summed, tiles.at[1], ey, 7, warped)
        return carry

    lax.fori_loop(0, 4, element, 0)
    middle = (lane >= 16) & (lane < 112)

    def rows(step, carry):
        y = pl.multiple_of(step * 8, 8)
        low = pltpu.roll(xlo[GROUP * PY:, :], (8 - step) % 8 * 16, 1)
        high = pltpu.roll(xhi[GROUP * PY:, :], (8 - step) % 8 * 16, 1)
        sums = [[None] * 6 for _ in range(3)]
        sums_r = [[None] * 3 for _ in range(2)]

        def add(where, k, i, term):
            where[k][i] = term if where[k][i] is None else where[k][i] + term

        for z in range(BZ):
            g, here = slopes(pad, low, high, z, y, lane)
            for p, (c, d) in enumerate(PAIRS):
                product = g[c] * g[d]
                for k in range(3):
                    add(sums, k, p, product * float(_SQ[k][z]))
            moved = jnp.where(middle, inside[z, pl.ds(y, 8), :], warped[z, pl.ds(y, 8), :])
            mismatch = here - moved
            for c in range(3):
                product = g[c] * mismatch
                for k in range(2):
                    add(sums_r, k, c, product * float(_LIN[k][z]))
        for k in range(3):
            for p in range(6):
                acc_k[k, pl.ds(p * BY + y, 8), :] = sums[k][p]
        for k in range(2):
            for c in range(3):
                acc_r[k, pl.ds(c * BY + y, 8), :] = sums_r[k][c]
        return carry

    lax.fori_loop(0, BY // 8, rows, 0)

    def contract(left, fields, right):
        half = jnp.dot(left[...], fields, precision=HI, preferred_element_type=F32)
        return jnp.dot(half, right[...], precision=HI, preferred_element_type=F32)

    packed = [jnp.zeros((8, BX), F32) for _ in range(5)]
    for k in range(3):
        full = contract(left_k, acc_k[k], right_k)
        kz = 1 if k == 2 else 0
        for q in range(9):
            ky, jy = (0, q) if q < 5 else (1, q - 5)
            rows_ = full[q * 8:q * 8 + 8]
            for kx in range(2):
                if kz == 0:
                    row, base = ky * 2 + kx, BLK * k
                elif ky == 1:
                    row, base = 1 - kx, 90
                else:
                    row, base = 2 + kx, 81
                source = 0 if kx == 0 else 9
                width = 9 if kx == 0 else 8
                part = jnp.where((lane >= source) & (lane < source + width), rows_, 0.0)
                packed[row] = packed[row] + roll(part, base + jy * JX - source)
    for k in range(2):
        full = contract(left_r, acc_r[k], right_r)
        for jy in range(JY):
            part = jnp.where(lane < JX, full[jy * 8:jy * 8 + 8], 0.0)
            packed[4] = packed[4] + roll(part, BLK * k + jy * JX)
    for row in range(4):
        out[row * 6:row * 6 + 6, :] = packed[row][0:6]
    out[KROWS:KROWS + 8, :] = packed[4]


def terms(summed, *arrays):
    return pl.pallas_call(
        terms_kernel,
        out_shape=jax.ShapeDtypeStruct((KROWS + 8, BX), F32),
        in_specs=[SMEM] + [VMEM] * 15,
        out_specs=VMEM,
        scratch_shapes=[
            pltpu.VMEM((BZ + 2, BY + 16, BX), F32),
            pltpu.VMEM((2, PZ, PY, BX), F32),
            pltpu.VMEM((BZ, BY, BX), F32),
            pltpu.VMEM((3, 6 * BY, BX), F32),
            pltpu.VMEM((2, 3 * BY, BX), F32),
        ],
        compiler_params=grant(20),
        name="terms",
    )(summed, *arrays, jnp.asarray(LEFT_K), jnp.asarray(RIGHT_K),
      jnp.asarray(LEFT_R), jnp.asarray(RIGHT_R))


NZ = NGZ + 1
TILES = NZ * 2


SLOTS0 = 54 * TILES
SLOTS = SLOTS0 + 54 * 2 * NGZ


STEPS = (("gz", (1, 2, 3), False), ("gx", (2,), False), ("gy", (2, 4, 6), False), ("gx", (1, 3), True))
QUAD = NGZ * (KROWS + RROWS)


def units():
    held = [(0, 0)]
    for axis, partners, halved in STEPS[1:]:
        n = len(held) // 2
        groups = (held[:n], held[n:]) if halved else (held,) * len(partners)
        for group, s in zip(groups, partners):
            dx, dy = (s, 0) if axis == "gx" else (0, s)
            held = held + [(x ^ dx, y ^ dy) for x, y in group]
    assert sorted(held) == [(x, y) for x in range(NGX) for y in range(0, NGY, 2)]
    return held


def brick(buf, where, gz, gx, row, rhs):
    dz, dx = gz ^ where[0], gx ^ where[2]
    first = NGZ * KROWS + dz * RROWS if rhs else dz * KROWS
    start = pl.multiple_of((((dx & 1) * 2 + (dx >> 1)) * QUAD + first + row) * 8, 8)
    return buf[pl.ds(start, 8), :]


def stencil_slot(kz, oy, ox, pair, i):
    slot = ((oy + 1) * 3 + ox + 1) * 6 + pair
    return slot * TILES + i if kz == 0 else SLOTS0 + slot * 2 * NGZ + i


def planes(s, width):
    lane = lanes()
    zero = jnp.zeros((8, BX), F32)
    out = []
    for z in range(NZ):
        for h in range(2):
            e, o = zero, zero
            if z < NGZ:
                e = s[z][2 * h]
                o = roll(s[z][2 * h + 1], BLK)
            if z > 0:
                e = e + roll(s[z - 1][2 * h], -BLK)
                o = o + s[z - 1][2 * h + 1]
            odd = (lane >= BLK) & (lane < BLK + width)
            out.append(jnp.where(lane < width, e, jnp.where(odd, o, zero)))
    return out


def edges(s, base, width):
    lane = lanes()
    out = []
    for z in range(NGZ):
        for h in range(2):
            e = roll(s[z][2 * h], -base)
            o = roll(s[z][2 * h + 1], BLK - base)
            odd = (lane >= BLK) & (lane < BLK + width)
            out.append(jnp.where(lane < width, e, jnp.where(odd, o, 0.0)))
    return out


def cg_kernel(
    where, part0, part1, out_x, out_r, buf, stencil, shifted, xs, rs, ys,
):
    own_z, own_y, own_x = where[0], where[1], where[2]
    for side, part in enumerate((part0, part1)):
        for i, (dx, dy) in enumerate(units()):
            gy = own_y ^ (side + dy)
            place = (dx & 1) * 2 + (dx >> 1)
            for r in range(0, QUAD, 8):
                buf[pl.ds((place * QUAD + r) * 8 + gy, 8, stride=8), :] = (
                    part[i * QUAD + r:i * QUAD + r + 8, :])

    def build(pair, carry):
        for row in range(4):
            s = [[brick(buf, where, gz, gx, row * 6 + pair, False) for gx in range(NGX)]
                 for gz in range(NGZ)]
            upper = (1, 1, 0, 0)[row]
            sides = (
                (0, row >> 1, row & 1, planes(s, 36 if row >> 1 else BLK)),
                (1, upper, (1, 0, 0, 1)[row],
                 edges(s, 90 if upper else 81, 36 if upper else BLK)),
            )
            for kz, ky, kx, field in sides:
                for oy in ((0,) if ky == 0 else (1, -1)):
                    for ox in ((0,) if kx == 0 else (1, -1)):
                        amount = (JX if oy == -1 else 0) + (1 if ox == 1 else 0)
                        for i, v in enumerate(field):
                            stencil[stencil_slot(kz, oy, ox, pair, i)] = roll(v, amount)
        return carry

    lax.fori_loop(0, 6, build, 0)
    lane = lanes()
    sub = lax.broadcasted_iota(jnp.int32, (8, BX), 0)
    even, odd = lane < BLK, (lane >= BLK) & (lane < 2 * BLK)
    zero = jnp.zeros((8, BX), F32)

    def fold(y0, y1):
        a = y0 + jnp.where(m_odd0, roll(y0, 37), 0.0) + jnp.where(m_even8, roll(y0, -37), 0.0)
        b = y1 + jnp.where(m_odd0, roll(y1, 37), 0.0) + jnp.where(m_even8, roll(y1, -37), 0.0)
        a = a + jnp.where(m_odd8, roll(y1, 53), 0.0)
        b = b + jnp.where(m_even0, roll(y0, -53), 0.0)
        out = []
        for v in (a, b):
            up = roll(roll(v, 36), 7, 0)
            down = roll(roll(v, -36), 1, 0)
            out.append(v + jnp.where(m_top, up, 0.0) + jnp.where(m_bottom, down, 0.0))
        return out

    inside = lax.rem(lane, BLK)
    jy = inside // JX
    jx = lax.rem(inside, JX)
    m_odd0, m_odd8 = odd & (jx == 0), odd & (jx == 8)
    m_even0, m_even8 = even & (jx == 0), even & (jx == 8)
    valid = lane < 2 * BLK
    m_top = valid & (jy == 4) & (sub < 7)
    m_bottom = valid & (jy == 0) & (sub > 0)
    base = valid & ((jy < 4) | (sub == 7))
    owner = (
        jnp.where(base & (jx < 8), 1.0, 0.0),
        jnp.where(base & ((jx < 8) | odd), 1.0, 0.0),
    )

    def total(v):
        return jnp.sum(jnp.sum(v, axis=1, keepdims=True), axis=0, keepdims=True)

    part = [zero, zero]
    for c in range(3):
        s = [[brick(buf, where, gz, gx, c, True) for gx in range(NGX)] for gz in range(NGZ)]
        field = planes(s, BLK)
        for z in range(NZ):
            pair_ = fold(field[2 * z], field[2 * z + 1])
            for h in range(2):
                v = pair_[h]
                i = 2 * z + h
                rs[c, i] = v
                xs[c, i] = zero
                shifted[c, 1, i] = v
                shifted[c, 0, i] = roll(v, JX)
                shifted[c, 2, i] = roll(v, -JX)
                part[h] = part[h] + v * v
    norm = total(part[0] * owner[0] + part[1] * owner[1])

    def step(_, norm_now):
        part = [zero, zero]
        for z in range(NZ):
            for h in range(2):
                sums = [[None] * 3 for _ in range(3)]
                for oz in (-1, 0, 1):
                    if not 0 <= z + oz < NZ:
                        continue
                    kz = 0 if oz == 0 else 1
                    kt = (z - 1 if oz == -1 else z) * 2 + h
                    for oy in range(3):
                        p = [shifted[d, oy, (z + oz) * 2 + h] for d in range(3)]
                        for ox in range(3):
                            k = [stencil[stencil_slot(kz, oy - 1, ox - 1, q, kt)] for q in range(6)]
                            for c in range(3):
                                for d in range(3):
                                    term = k[PAIR_OF[min(c, d), max(c, d)]] * p[d]
                                    old = sums[c][ox]
                                    sums[c][ox] = term if old is None else old + term
                for c in range(3):
                    ys[c, 2 * z + h] = sums[c][1] + roll(sums[c][0], 1) + roll(sums[c][2], -1)
            for c in range(3):
                pair_ = fold(ys[c, 2 * z], ys[c, 2 * z + 1])
                for h in range(2):
                    i = 2 * z + h
                    p = shifted[c, 1, i]
                    v = pair_[h] + DAMPING * p
                    ys[c, i] = v
                    part[h] = part[h] + v * p
        alpha = norm_now / total(part[0] * owner[0] + part[1] * owner[1])
        part = [zero, zero]
        for c in range(3):
            for i in range(TILES):
                xs[c, i] = xs[c, i] + alpha * shifted[c, 1, i]
                r = rs[c, i] - alpha * ys[c, i]
                rs[c, i] = r
                part[i % 2] = part[i % 2] + r * r
        norm_next = total(part[0] * owner[0] + part[1] * owner[1])
        beta = norm_next / norm_now
        for c in range(3):
            for i in range(TILES):
                p = rs[c, i] + beta * shifted[c, 1, i]
                shifted[c, 1, i] = p
                shifted[c, 0, i] = roll(p, JX)
                shifted[c, 2, i] = roll(p, -JX)
        return norm_next

    lax.fori_loop(0, CGSTEPS, step, norm)

    half, side = own_x >> 1, own_x & 1
    turn = jnp.where(side == 1, BX - BLK, 0)
    for src, dst, scale in ((xs, out_x, float(QUANTUM)), (rs, out_r, 1.0)):
        for c in range(3):
            for jz in range(2):
                v = src[c, (own_z + jz) * 2 + half]
                v = pltpu.roll(pltpu.roll(v, turn, 1), (8 - own_y) & 7, 0) * scale
                tile = zero
                for j in range(JY):
                    row = roll(roll(v, -j * JX), j, 0)
                    tile = jnp.where(sub == j, row, tile)
                dst[c, :, jz, :] = tile[0:JY, 0:JX]


def solve(where, parts):
    shape = jax.ShapeDtypeStruct((3, JY, 2, JX), F32)
    field = pltpu.VMEM((3, TILES, 8, BX), F32)
    return pl.pallas_call(
        cg_kernel,
        out_shape=[shape, shape],
        in_specs=[SMEM] + [VMEM] * 2,
        out_specs=[VMEM, VMEM],
        scratch_shapes=[
            pltpu.VMEM((NGX * QUAD * 8, BX), F32),
            pltpu.VMEM((SLOTS, 8, BX), F32),
            pltpu.VMEM((3, 3, TILES, 8, BX), F32),
            field, field, field,
        ],
        compiler_params=grant(20),
        name="cg",
    )(where, *parts)


def partner(x, axis, s):
    return lax.ppermute(x, axis, [(k ^ s, k) for k in range(lax.axis_size(axis))])


def exchange(a, b, axis):
    n = lax.axis_size(axis)
    outer = [(k, k + 1) for k in range(1, n - 1, 2)]
    b = lax.ppermute(b, axis, outer + [(j, i) for i, j in outer])
    return partner(a, axis, 1), b


def sorted_sides(a, b, axis):
    even = lax.axis_index(axis) % 2 == 0
    return jnp.where(even, b, a), jnp.where(even, a, b)


def halo(low, high, axis):
    even = lax.axis_index(axis) % 2 == 0
    return sorted_sides(
        *exchange(jnp.where(even, high, low), jnp.where(even, low, high), axis), axis)


def along_y(up, down):
    even = lax.axis_index("gy") % 2 == 0
    out = [(k, k + 1) for k in range(1, NGY - 1, 2)]
    near = [(k, k ^ 1) for k in range(NGY)]
    outer = jnp.where(even, down, up)
    up, down, _ = lax.optimization_barrier((up, down, outer))
    outer = lax.ppermute(outer, "gy", out + [(b, a) for a, b in out])
    inner_ = lax.ppermute(jnp.where(even, up, down), "gy", near)
    return jnp.where(even, outer, inner_), jnp.where(even, inner_, outer)


def gather(rows):
    for i, (axis, partners, halved) in enumerate(STEPS):
        n = rows.shape[0] // 2
        held = (rows[:n], rows[n:]) if halved else (rows,) * len(partners)
        theirs = [partner(h, axis, s) for h, s in zip(held, partners)]
        if i == 0:
            k, r = KROWS, KROWS + RROWS
            theirs = [v[:k] for v in [rows] + theirs] + [v[k:r] for v in [rows] + theirs]
            rows = jnp.concatenate(theirs, 0)
        else:
            rows = jnp.concatenate([rows] + theirs, 0)
    return rows, partner(rows, "gy", 1)


def element_sums(nodes):
    low = nodes[:, 0] + nodes[:, 1]
    low = low[:, :-1] + low[:, 1:]
    low = low[:, :, :-1] + low[:, :, 1:]
    return low.reshape(96)


def per_device(ref_image, deformed_image, nodal_disp):
    dza, dzb = exchange(deformed_image, deformed_image, "gz")
    rzlo, rzhi = halo(ref_image[:1], ref_image[BZ - 1:], "gz")
    summed = element_sums(nodal_disp)
    where = jnp.stack([lax.axis_index("gz"), lax.axis_index("gy"), lax.axis_index("gx")])
    dza, dzb, rzlo, rzhi, summed = lax.optimization_barrier((dza, dzb, rzlo, rzhi, summed))
    dzlo, dzhi = sorted_sides(dza, dzb, "gz")
    planes_ = (dzlo, deformed_image, dzhi)
    up = [v[:, BY - E:, :] for v in planes_] + [ref_image[:, BY - 1, :][None]]
    down = [v[:, :E, :] for v in planes_] + [ref_image[:, 0, :][None]]
    dylo, dyhi = along_y(jnp.concatenate(up, 0), jnp.concatenate(down, 0))
    blocks = (deformed_image, dzlo, dzhi, dylo, dyhi)
    first, last = strips(ref_image, *blocks)
    dxlo, dxhi = halo(first, last, "gx")
    inside = inner(lax.optimization_barrier((summed, first))[0], *blocks)
    rows = terms(summed, ref_image, rzlo, rzhi, *blocks, dxlo, dxhi, inside)
    return tuple(jnp.swapaxes(v, 1, 2) for v in solve(where, gather(rows)))


def solution(mesh):
    spec3 = P("gz", "gy", "gx")
    spec4 = P(None, "gz", "gy", "gx")
    return jax.shard_map(
        per_device, mesh=mesh, in_specs=(spec3, spec3, spec4), out_specs=(spec4, spec4),
        check_vma=False,
    )
```

profile of v0, /device:TPU:1, one launch (start us, length us, event | category | flops | bytes accessed | tf_op | source)
XLA Modules:
  0.0 93.8 jit_solution(16681417963229996043)
XLA Ops:
  0.6 0.7 collective-permute-start.1
  1.3 5.4 %collective-permute-start = (f32[16,64,128]{2,1,0:T(8,128)}, f32[16,64,128]{2,1,0:T(8,128)S(1)}, u32[]{:S(2)}, u32[]{:S(2)}) collective-permute-start(f32[16,64,128]{2,1,0:T(8,128)} %mid.5), channel_id=1, source_target_pairs={{32,0},{0,32},{96,64},{64,96},{33,1},{1,33},{97,65},{65,97},{34,2}... | collective-permute-start | bytes 1572872 | tf_op jit(solution)/shard_map/ppermute | solution.py:550
  6.7 0.8 slice_select_fusion
  7.5 0.7 collective-permute-start.2
  8.2 0.9 fusion.3
  9.1 1.0 %fusion.1 = (f32[16,16,128]{2,1,0:T(8,128)S(1)}, f32[16,16,128]{2,1,0:T(8,128)S(1)}) fusion(f32[16,64,128]{2,1,0:T(8,128)} %mid.5), kind=kLoop, calls=%fused_computation.23 | loop fusion | bytes 524288 | tf_op jit(solution)/shard_map/slice | solution.py:612
  10.3 8.7 %collective-permute-done.3 = f32[1,64,128]{2,1,0:T(8,128)S(1)} collective-permute-done((f32[1,64,128]{2,1,0:T(8,128)S(1)}, f32[1,64,128]{2,1,0:T(8,128)S(1)}, u32[]{:S(2)}, u32[]{:S(2)}) %collective-permute-start.3) | collective-permute-done | bytes 32800 | tf_op jit(solution)/shard_map/ppermute | solution.py:550
  19.3 1.6 %collective-permute-start.5 = (f32[49,16,128]{2,1,0:T(8,128)S(1)}, f32[49,16,128]{2,1,0:T(8,128)S(1)}, u32[]{:S(2)}, u32[]{:S(2)}) collective-permute-start(f32[49,16,128]{2,1,0:T(8,128)S(1)} %broadcast_select_fusion.4), channel_id=1, source_target_pairs={{0,4},{4,0},{8,12},{12,8},{16,20},{20,16},{24,28},{28,24},{1,5},{5... | collective-permute-start | bytes 1204232 | tf_op jit(solution)/shard_map/ppermute | solution.py:578
  20.9 3.1 %collective-permute-start.4 = (f32[49,16,128]{2,1,0:T(8,128)S(1)}, f32[49,16,128]{2,1,0:T(8,128)S(1)}, u32[]{:S(2)}, u32[]{:S(2)}) collective-permute-start(f32[49,16,128]{2,1,0:T(8,128)S(1)} %get-tuple-element.45), channel_id=1, source_target_pairs={{4,8},{12,16},{20,24},{8,4},{16,12},{24,20},{5,9},{13,17},{21,25},... | collective-permute-start | bytes 1204232 | tf_op jit(solution)/shard_map/ppermute | solution.py:577
  24.1 6.1 %collective-permute-done.4 = f32[49,16,128]{2,1,0:T(8,128)S(1)} collective-permute-done((f32[49,16,128]{2,1,0:T(8,128)S(1)}, f32[49,16,128]{2,1,0:T(8,128)S(1)}, u32[]{:S(2)}, u32[]{:S(2)}) %collective-permute-start.4) | collective-permute-done | bytes 401440 | tf_op jit(solution)/shard_map/ppermute | solution.py:577
  30.3 0.9 strips.1
  31.2 1.5 %collective-permute-start.7 = (f32[584,128]{1,0:T(8,128)S(1)}, f32[584,128]{1,0:T(8,128)S(1)}, u32[]{:S(2)}, u32[]{:S(2)}) collective-permute-start(f32[584,128]{1,0:T(8,128)S(1)} %get-tuple-element.32), channel_id=1, source_target_pairs={{1,0},{0,1},{3,2},{2,3},{5,4},{4,5},{7,6},{6,7},{9,8},{8,9},{11,10... | collective-permute-start | bytes 897032 | tf_op jit(solution)/shard_map/ppermute | solution.py:550
  32.7 0.7 collective-permute-start.6
  33.4 3.7 %inner.1.inside = f32[16,64,128]{2,1,0:T(8,128)S(1)} custom-call(s32[96]{0:T(128)S(1)} %reshape.8.summed, f32[16,64,128]{2,1,0:T(8,128)S(1)} %copy-done, f32[16,64,128]{2,1,0:T(8,128)S(1)} %get-tuple-element.27.zlo, f32[16,64,128]{2,1,0:T(8,128)S(1)} %get-tuple-element.26.zhi, f32[49,16,128]{2,1,0:T(8,128)S(1)} %get-tuple-element.29.ylo, ...), custom_call_target="tpu_custom_call" | custom-call | tf_op jit(solution)/shard_map/inner/pallas_call | solution.py:186
  37.2 0.8 copy-done.2
  38.0 5.8 %terms.1 = f32[32,128]{1,0:T(8,128)S(1)} custom-call(s32[96]{0:T(128)S(1)} %reshape.8.summed, f32[16,64,128]{2,1,0:T(8,128)S(1)} %copy-done.1, f32[1,64,128]{2,1,0:T(8,128)S(1)} %get-tuple-element.15.rzlo, f32[1,64,128]{2,1,0:T(8,128)S(1)} %get-tuple-element.16.rzhi, f32[16,64,128]{2,1,0:T(8,128)S(1)} %copy-done, f32[16,64,128]{2,1,0:T(8,128)S(1)} %get-tuple-element.27.zlo, ...), custom_call_target="tpu_custom_call" | custom-call | tf_op jit(solution)/shard_map/terms/pallas_call | solution.py:301
  43.8 0.8 collective-permute-start.10
  44.5 2.5 %collective-permute-start.9 = (f32[32,128]{1,0:T(8,128)S(1)}, f32[32,128]{1,0:T(8,128)S(1)}, u32[]{:S(2)}, u32[]{:S(2)}) collective-permute-start(f32[32,128]{1,0:T(8,128)S(1)} %terms.1), channel_id=1, source_target_pairs={{64,0},{96,32},{0,64},{32,96},{65,1},{97,33},{1,65},{33,97},{66,2}... | collective-permute-start | bytes 49160 | tf_op jit(solution)/shard_map/ppermute | solution.py:550
  47.1 0.5 collective-permute-done.10
  47.6 1.0 %collective-permute-done.9 = f32[32,128]{1,0:T(8,128)S(1)} collective-permute-done((f32[32,128]{1,0:T(8,128)S(1)}, f32[32,128]{1,0:T(8,128)S(1)}, u32[]{:S(2)}, u32[]{:S(2)}) %collective-permute-start.9) | collective-permute-done | bytes 16416 | tf_op jit(solution)/shard_map/ppermute | solution.py:550
  48.6 1.0 %collective-permute-done.8 = f32[32,128]{1,0:T(8,128)S(1)} collective-permute-done((f32[32,128]{1,0:T(8,128)S(1)}, f32[32,128]{1,0:T(8,128)S(1)}, u32[]{:S(2)}, u32[]{:S(2)}) %collective-permute-start.8) | collective-permute-done | bytes 16416 | tf_op jit(solution)/shard_map/ppermute | solution.py:550
  49.7 4.6 %collective-permute-start.11 = (f32[112,128]{1,0:T(8,128)S(1)}, f32[112,128]{1,0:T(8,128)S(1)}, u32[]{:S(2)}, u32[]{:S(2)}) collective-permute-start(f32[112,128]{1,0:T(8,128)S(1)} %concatenate.27), channel_id=1, source_target_pairs={{2,0},{3,1},{0,2},{1,3},{6,4},{7,5},{4,6},{5,7},{10,8},{11,9},{8,1... | collective-permute-start | bytes 172040 | tf_op jit(solution)/shard_map/ppermute | solution.py:550
  54.3 1.6 %collective-permute-done.11 = f32[112,128]{1,0:T(8,128)S(1)} collective-permute-done((f32[112,128]{1,0:T(8,128)S(1)}, f32[112,128]{1,0:T(8,128)S(1)}, u32[]{:S(2)}, u32[]{:S(2)}) %collective-permute-start.11) | collective-permute-done | bytes 57376 | tf_op jit(solution)/shard_map/ppermute | solution.py:550
  56.0 6.0 %collective-permute-start.13 = (f32[224,128]{1,0:T(8,128)S(1)}, f32[224,128]{1,0:T(8,128)S(1)}, u32[]{:S(2)}, u32[]{:S(2)}) collective-permute-start(f32[224,128]{1,0:T(8,128)S(1)} %concatenate.28), channel_id=1, source_target_pairs={{16,0},{20,4},{24,8},{28,12},{0,16},{4,20},{8,24},{12,28},{17,1},{... | collective-permute-start | bytes 344072 | tf_op jit(solution)/shard_map/ppermute | solution.py:550
  62.0 2.2 %collective-permute-done.13 = f32[224,128]{1,0:T(8,128)S(1)} collective-permute-done((f32[224,128]{1,0:T(8,128)S(1)}, f32[224,128]{1,0:T(8,128)S(1)}, u32[]{:S(2)}, u32[]{:S(2)}) %collective-permute-start.13) | collective-permute-done | bytes 114720 | tf_op jit(solution)/shard_map/ppermute | solution.py:550
  64.2 1.0 %collective-permute-start.16 = (f32[448,128]{1,0:T(8,128)S(1)}, f32[448,128]{1,0:T(8,128)S(1)}, u32[]{:S(2)}, u32[]{:S(2)}) collective-permute-start(f32[448,128]{1,0:T(8,128)S(1)} %pad_maximum_fusion.2), channel_id=1, source_target_pairs={{3,0},{2,1},{1,2},{0,3},{7,4},{6,5},{5,6},{4,7},{11,8},{10,9},{9,1... | collective-permute-start | bytes 688136 | tf_op jit(solution)/shard_map/ppermute | solution.py:550
  65.3 0.4 collective-permute-done.12
  65.8 1.6 %collective-permute-start.15 = (f32[448,128]{1,0:T(8,128)S(1)}, f32[448,128]{1,0:T(8,128)S(1)}, u32[]{:S(2)}, u32[]{:S(2)}) collective-permute-start(f32[448,128]{1,0:T(8,128)S(1)} %concatenate.29), channel_id=1, source_target_pairs={{1,0},{0,1},{3,2},{2,3},{5,4},{4,5},{7,6},{6,7},{9,8},{8,9},{11,10... | collective-permute-start | bytes 688136 | tf_op jit(solution)/shard_map/ppermute | solution.py:550
  67.3 3.1 %collective-permute-done.16 = f32[448,128]{1,0:T(8,128)S(1)} collective-permute-done((f32[448,128]{1,0:T(8,128)S(1)}, f32[448,128]{1,0:T(8,128)S(1)}, u32[]{:S(2)}, u32[]{:S(2)}) %collective-permute-start.16) | collective-permute-done | bytes 229408 | tf_op jit(solution)/shard_map/ppermute | solution.py:550
  70.8 6.3 %collective-permute-start.17 = (f32[1792,128]{1,0:T(8,128)S(1)}, f32[1792,128]{1,0:T(8,128)S(1)}, u32[]{:S(2)}, u32[]{:S(2)}) collective-permute-start(f32[1792,128]{1,0:T(8,128)S(1)} %concatenate.31.part0), channel_id=1, source_target_pairs={{4,0},{0,4},{12,8},{8,12},{20,16},{16,20},{28,24},{24,28},{5,1},{1... | collective-permute-start | bytes 2752520 | tf_op jit(solution)/shard_map/ppermute | solution.py:550
  77.2 2.0 %collective-permute-done.17.part1 = f32[1792,128]{1,0:T(8,128)S(1)} collective-permute-done((f32[1792,128]{1,0:T(8,128)S(1)}, f32[1792,128]{1,0:T(8,128)S(1)}, u32[]{:S(2)}, u32[]{:S(2)}) %collective-permute-start.17) | collective-permute-done | bytes 917536 | tf_op jit(solution)/shard_map/ppermute | solution.py:550
  79.2 14.6 %cg.1 = (f32[3,5,2,9]{3,2,1,0:T(2,128)}, f32[3,5,2,9]{3,2,1,0:T(2,128)}) custom-call(s32[3]{0:T(128)S(1)} %pad_add_fusion.where, f32[1792,128]{1,0:T(8,128)S(1)} %concatenate.31.part0, f32[1792,128]{1,0:T(8,128)S(1)} %collective-permute-done.17.part1), custom_call_target="tpu_custom_call" | custom-call | tf_op jit(solution)/shard_map/cg/pallas_call | solution.py:533
  (53 shorter events, 1.5 us)
Async XLA Ops:
  0.6 18.4 %collective-permute-start.1 = (f32[16,64,128]{2,1,0:T(8,128)}, f32[16,64,128]{2,1,0:T(8,128)S(1)}, u32[]{:S(2)}, u32[]{:S(2)}) collective-permute-start(f32[16,64,128]{2,1,0:T(8,128)} %mid.5), channel_id=1, source_target_pairs={{32,64},{64,32},{33,65},{65,33},{34,66},{66,34},{35,67},{67,35},{3... | collective-permute-start | bytes 1572872 | tf_op jit(solution)/shard_map/ppermute | solution.py:556
  1.3 17.7 %collective-permute-start = (f32[16,64,128]{2,1,0:T(8,128)}, f32[16,64,128]{2,1,0:T(8,128)S(1)}, u32[]{:S(2)}, u32[]{:S(2)}) collective-permute-start(f32[16,64,128]{2,1,0:T(8,128)} %mid.5), channel_id=1, source_target_pairs={{32,0},{0,32},{96,64},{64,96},{33,1},{1,33},{97,65},{65,97},{34,2}... | collective-permute-start | bytes 1572872 | tf_op jit(solution)/shard_map/ppermute | solution.py:550
  7.5 11.5 %collective-permute-start.3 = (f32[1,64,128]{2,1,0:T(8,128)S(1)}, f32[1,64,128]{2,1,0:T(8,128)S(1)}, u32[]{:S(2)}, u32[]{:S(2)}) collective-permute-start(f32[1,64,128]{2,1,0:T(8,128)S(1)} %get-tuple-element.42), channel_id=1, source_target_pairs={{32,0},{0,32},{96,64},{64,96},{33,1},{1,33},{97,65},{65,97},{34,2}... | collective-permute-start | bytes 98312 | tf_op jit(solution)/shard_map/ppermute | solution.py:550
  7.5 11.4 %collective-permute-start.2 = (f32[1,64,128]{2,1,0:T(8,128)S(1)}, f32[1,64,128]{2,1,0:T(8,128)S(1)}, u32[]{:S(2)}, u32[]{:S(2)}) collective-permute-start(f32[1,64,128]{2,1,0:T(8,128)S(1)} %get-tuple-element.43), channel_id=1, source_target_pairs={{32,64},{64,32},{33,65},{65,33},{34,66},{66,34},{35,67},{67,35},{3... | collective-permute-start | bytes 98312 | tf_op jit(solution)/shard_map/ppermute | solution.py:556
  9.1 1.0 %copy-start.6 = (s32[3,2,5,9]{3,1,2,0:T(2,128)S(1)}, s32[3,2,5,9]{3,1,2,0:T(2,128)}, u32[]{:S(2)}) copy-start(s32[3,2,5,9]{3,1,2,0:T(2,128)} %param.9) | copy-start | bytes 3244
  19.3 4.8 %collective-permute-start.5 = (f32[49,16,128]{2,1,0:T(8,128)S(1)}, f32[49,16,128]{2,1,0:T(8,128)S(1)}, u32[]{:S(2)}, u32[]{:S(2)}) collective-permute-start(f32[49,16,128]{2,1,0:T(8,128)S(1)} %broadcast_select_fusion.4), channel_id=1, source_target_pairs={{0,4},{4,0},{8,12},{12,8},{16,20},{20,16},{24,28},{28,24},{1,5},{5... | collective-permute-start | bytes 1204232 | tf_op jit(solution)/shard_map/ppermute | solution.py:578
  20.9 9.3 %collective-permute-start.4 = (f32[49,16,128]{2,1,0:T(8,128)S(1)}, f32[49,16,128]{2,1,0:T(8,128)S(1)}, u32[]{:S(2)}, u32[]{:S(2)}) collective-permute-start(f32[49,16,128]{2,1,0:T(8,128)S(1)} %get-tuple-element.45), channel_id=1, source_target_pairs={{4,8},{12,16},{20,24},{8,4},{16,12},{24,20},{5,9},{13,17},{21,25},... | collective-permute-start | bytes 1204232 | tf_op jit(solution)/shard_map/ppermute | solution.py:577
  24.1 6.2 %copy-start = (f32[16,64,128]{2,1,0:T(8,128)S(1)}, f32[16,64,128]{2,1,0:T(8,128)}, u32[]{:S(2)}) copy-start(f32[16,64,128]{2,1,0:T(8,128)} %mid.5) | copy-start | bytes 1572868
  24.1 6.2 %copy-start.1 = (f32[16,64,128]{2,1,0:T(8,128)S(1)}, f32[16,64,128]{2,1,0:T(8,128)}, u32[]{:S(2)}) copy-start(f32[16,64,128]{2,1,0:T(8,128)} %ref.3) | copy-start | bytes 1572868
  31.2 5.9 %collective-permute-start.7 = (f32[584,128]{1,0:T(8,128)S(1)}, f32[584,128]{1,0:T(8,128)S(1)}, u32[]{:S(2)}, u32[]{:S(2)}) collective-permute-start(f32[584,128]{1,0:T(8,128)S(1)} %get-tuple-element.32), channel_id=1, source_target_pairs={{1,0},{0,1},{3,2},{2,3},{5,4},{4,5},{7,6},{6,7},{9,8},{8,9},{11,10... | collective-permute-start | bytes 897032 | tf_op jit(solution)/shard_map/ppermute | solution.py:550
  32.7 4.4 %collective-permute-start.6 = (f32[584,128]{1,0:T(8,128)S(1)}, f32[584,128]{1,0:T(8,128)S(1)}, u32[]{:S(2)}, u32[]{:S(2)}) collective-permute-start(f32[584,128]{1,0:T(8,128)S(1)} %get-tuple-element.33), channel_id=1, source_target_pairs={{1,2},{2,1},{5,6},{6,5},{9,10},{10,9},{13,14},{14,13},{17,18},{18,... | collective-permute-start | bytes 897032 | tf_op jit(solution)/shard_map/ppermute | solution.py:556
  37.1 0.9 copy-start.2
  37.1 0.9 copy-start.3
  37.1 0.9 copy-start.4
  37.1 0.9 copy-start.5
  43.8 3.8 %collective-permute-start.10 = (f32[32,128]{1,0:T(8,128)S(1)}, f32[32,128]{1,0:T(8,128)S(1)}, u32[]{:S(2)}, u32[]{:S(2)}) collective-permute-start(f32[32,128]{1,0:T(8,128)S(1)} %terms.1), channel_id=1, source_target_pairs={{96,0},{64,32},{32,64},{0,96},{97,1},{65,33},{33,65},{1,97},{98,2}... | collective-permute-start | bytes 49160 | tf_op jit(solution)/shard_map/ppermute | solution.py:550
  44.5 4.1 %collective-permute-start.9 = (f32[32,128]{1,0:T(8,128)S(1)}, f32[32,128]{1,0:T(8,128)S(1)}, u32[]{:S(2)}, u32[]{:S(2)}) collective-permute-start(f32[32,128]{1,0:T(8,128)S(1)} %terms.1), channel_id=1, source_target_pairs={{64,0},{96,32},{0,64},{32,96},{65,1},{97,33},{1,65},{33,97},{66,2}... | collective-permute-start | bytes 49160 | tf_op jit(solution)/shard_map/ppermute | solution.py:550
  47.1 2.6 %collective-permute-start.8 = (f32[32,128]{1,0:T(8,128)S(1)}, f32[32,128]{1,0:T(8,128)S(1)}, u32[]{:S(2)}, u32[]{:S(2)}) collective-permute-start(f32[32,128]{1,0:T(8,128)S(1)} %terms.1), channel_id=1, source_target_pairs={{32,0},{0,32},{96,64},{64,96},{33,1},{1,33},{97,65},{65,97},{34,2}... | collective-permute-start | bytes 49160 | tf_op jit(solution)/shard_map/ppermute | solution.py:550
  49.7 6.2 %collective-permute-start.11 = (f32[112,128]{1,0:T(8,128)S(1)}, f32[112,128]{1,0:T(8,128)S(1)}, u32[]{:S(2)}, u32[]{:S(2)}) collective-permute-start(f32[112,128]{1,0:T(8,128)S(1)} %concatenate.27), channel_id=1, source_target_pairs={{2,0},{3,1},{0,2},{1,3},{6,4},{7,5},{4,6},{5,7},{10,8},{11,9},{8,1... | collective-permute-start | bytes 172040 | tf_op jit(solution)/shard_map/ppermute | solution.py:550
  56.0 6.1 %collective-permute-start.14 = (f32[224,128]{1,0:T(8,128)S(1)}, f32[224,128]{1,0:T(8,128)S(1)}, u32[]{:S(2)}, u32[]{:S(2)}) collective-permute-start(f32[224,128]{1,0:T(8,128)S(1)} %concatenate.28), channel_id=1, source_target_pairs={{24,0},{28,4},{16,8},{20,12},{8,16},{12,20},{0,24},{4,28},{25,1},{... | collective-permute-start | bytes 344072 | tf_op jit(solution)/shard_map/ppermute | solution.py:550
  56.0 8.2 %collective-permute-start.13 = (f32[224,128]{1,0:T(8,128)S(1)}, f32[224,128]{1,0:T(8,128)S(1)}, u32[]{:S(2)}, u32[]{:S(2)}) collective-permute-start(f32[224,128]{1,0:T(8,128)S(1)} %concatenate.28), channel_id=1, source_target_pairs={{16,0},{20,4},{24,8},{28,12},{0,16},{4,20},{8,24},{12,28},{17,1},{... | collective-permute-start | bytes 344072 | tf_op jit(solution)/shard_map/ppermute | solution.py:550
  62.0 3.7 %collective-permute-start.12 = (f32[224,128]{1,0:T(8,128)S(1)}, f32[224,128]{1,0:T(8,128)S(1)}, u32[]{:S(2)}, u32[]{:S(2)}) collective-permute-start(f32[224,128]{1,0:T(8,128)S(1)} %concatenate.28), channel_id=1, source_target_pairs={{8,0},{12,4},{0,8},{4,12},{24,16},{28,20},{16,24},{20,28},{9,1},{1... | collective-permute-start | bytes 344072 | tf_op jit(solution)/shard_map/ppermute | solution.py:550
  64.2 6.2 %collective-permute-start.16 = (f32[448,128]{1,0:T(8,128)S(1)}, f32[448,128]{1,0:T(8,128)S(1)}, u32[]{:S(2)}, u32[]{:S(2)}) collective-permute-start(f32[448,128]{1,0:T(8,128)S(1)} %pad_maximum_fusion.2), channel_id=1, source_target_pairs={{3,0},{2,1},{1,2},{0,3},{7,4},{6,5},{5,6},{4,7},{11,8},{10,9},{9,1... | collective-permute-start | bytes 688136 | tf_op jit(solution)/shard_map/ppermute | solution.py:550
  65.8 5.0 %collective-permute-start.15 = (f32[448,128]{1,0:T(8,128)S(1)}, f32[448,128]{1,0:T(8,128)S(1)}, u32[]{:S(2)}, u32[]{:S(2)}) collective-permute-start(f32[448,128]{1,0:T(8,128)S(1)} %concatenate.29), channel_id=1, source_target_pairs={{1,0},{0,1},{3,2},{2,3},{5,4},{4,5},{7,6},{6,7},{9,8},{8,9},{11,10... | collective-permute-start | bytes 688136 | tf_op jit(solution)/shard_map/ppermute | solution.py:550
  70.8 8.4 %collective-permute-start.17 = (f32[1792,128]{1,0:T(8,128)S(1)}, f32[1792,128]{1,0:T(8,128)S(1)}, u32[]{:S(2)}, u32[]{:S(2)}) collective-permute-start(f32[1792,128]{1,0:T(8,128)S(1)} %concatenate.31.part0), channel_id=1, source_target_pairs={{4,0},{0,4},{12,8},{8,12},{20,16},{16,20},{28,24},{24,28},{5,1},{1... | collective-permute-start | bytes 2752520 | tf_op jit(solution)/shard_map/ppermute | solution.py:550
where the time goes:
time: 94.9 us; the launch traced here: 93.8 us
  starting transfers between devices  36.5 us (38%)
  waiting for transfers between devices  27 us (28%)
  Pallas kernels  25 us (26%)
  local copies, waits for them, and re-layouts  3.09 us (3%)
  other arithmetic  1.37 us (1%)
    ppermute x13, starting transfers between devices, partner(): lax.ppermute(x, axis, [(k ^ s, k) for k in range(lax.axis_size(axis))])  29.8 us
    ppermute x13, waiting for transfers between devices, partner(): lax.ppermute(x, axis, [(k ^ s, k) for k in range(lax.axis_size(axis))])  20.9 us
    pallas_call x1, Pallas kernels, solve(): pl.pallas_call(cg_kernel, out_shape=[shape, shape], in_specs=[SMEM] + [VM...  14.6 us
    ppermute x1, waiting for transfers between devices, along_y(): outer = lax.ppermute(outer, 'gy', out + [(b, a) for a, b in out])  6.14 us
    pallas_call x1, Pallas kernels, terms(): pl.pallas_call(terms_kernel, out_shape=jax.ShapeDtypeStruct((KROWS + 8, B...  5.77 us
    pallas_call x1, Pallas kernels, inner(): pl.pallas_call(inner_kernel, out_shape=jax.ShapeDtypeStruct((BZ, BY, BX),...  3.72 us
    ppermute x1, starting transfers between devices, along_y(): outer = lax.ppermute(outer, 'gy', out + [(b, a) for a, b in out])  3.1 us
    ppermute x3, starting transfers between devices, exchange(): b = lax.ppermute(b, axis, outer + [(j, i) for i, j in outer])  2.01 us
  transfers between devices with their start and end apart: 18, of which 11 were waited for; matrix products, arithmetic and copies ran while one was open for 3% of the time, Pallas kernels for 4%

commit v1 on v0

--- a/solution.py
+++ b/solution.py
@@ -265,13 +265,19 @@
 
     lax.fori_loop(0, BY // 8, rows, 0)
 
-    def contract(left, fields, right):
-        half = jnp.dot(left[...], fields, precision=HI, preferred_element_type=F32)
-        return jnp.dot(half, right[...], precision=HI, preferred_element_type=F32)
-
+    def contract(left, fields, count, right):
+        halves = [jnp.dot(left[...], fields[k], precision=HI, preferred_element_type=F32)
+                  for k in range(count)]
+        full = jnp.dot(jnp.concatenate(halves, 0), right[...], precision=HI,
+                       preferred_element_type=F32)
+        n = left.shape[0]
+        return [full[k * n:k * n + n] for k in range(count)]
+
+    fulls_k = contract(left_k, acc_k, 3, right_k)
+    fulls_r = contract(left_r, acc_r, 2, right_r)
     packed = [jnp.zeros((8, BX), F32) for _ in range(5)]
     for k in range(3):
-        full = contract(left_k, acc_k[k], right_k)
+        full = fulls_k[k]
         kz = 1 if k == 2 else 0
         for q in range(9):
             ky, jy = (0, q) if q < 5 else (1, q - 5)
@@ -288,7 +294,7 @@
                 part = jnp.where((lane >= source) & (lane < source + width), rows_, 0.0)
                 packed[row] = packed[row] + roll(part, base + jy * JX - source)
     for k in range(2):
-        full = contract(left_r, acc_r[k], right_r)
+        full = fulls_r[k]
         for jy in range(JY):
             part = jnp.where(lane < JX, full[jy * 8:jy * 8 + 8], 0.0)
             packed[4] = packed[4] + roll(part, BLK * k + jy * JX)

time: 94.9 us -> 94.5 us (level)
  no operation moved by 1% of the time
where the time goes in v1:
time: 94.5 us; the launch traced here: 93.4 us
  starting transfers between devices  36.6 us (39%)
  waiting for transfers between devices  27 us (29%)
  Pallas kernels  24.5 us (26%)
  local copies, waits for them, and re-layouts  3.09 us (3%)
  other arithmetic  1.37 us (1%)
    ppermute x13, starting transfers between devices, partner(): lax.ppermute(x, axis, [(k ^ s, k) for k in range(lax.axis_size(axis))])  29.8 us
    ppermute x13, waiting for transfers between devices, partner(): lax.ppermute(x, axis, [(k ^ s, k) for k in range(lax.axis_size(axis))])  20.9 us
    pallas_call x1, Pallas kernels, solve(): pl.pallas_call(cg_kernel, out_shape=[shape, shape], in_specs=[SMEM] + [VM...  14.6 us
    ppermute x1, waiting for transfers between devices, along_y(): outer = lax.ppermute(outer, 'gy', out + [(b, a) for a, b in out])  6.14 us
    pallas_call x1, Pallas kernels, terms(): pl.pallas_call(terms_kernel, out_shape=jax.ShapeDtypeStruct((KROWS + 8, B...  5.28 us
    pallas_call x1, Pallas kernels, inner(): pl.pallas_call(inner_kernel, out_shape=jax.ShapeDtypeStruct((BZ, BY, BX),...  3.72 us
    ppermute x1, starting transfers between devices, along_y(): outer = lax.ppermute(outer, 'gy', out + [(b, a) for a, b in out])  3.1 us
    ppermute x3, starting transfers between devices, exchange(): b = lax.ppermute(b, axis, outer + [(j, i) for i, j in outer])  2.01 us
  transfers between devices with their start and end apart: 18, of which 11 were waited for; matrix products, arithmetic and copies ran while one was open for 3% of the time, Pallas kernels for 4%

profile of v1, /device:TPU:1, one launch (start us, length us, event | category | flops | bytes accessed | tf_op | source)
XLA Modules:
  0.0 93.4 jit_solution(6934085768022594417)
XLA Ops:
  0.6 0.7 collective-permute-start.1
  1.3 5.4 %collective-permute-start = (f32[16,64,128]{2,1,0:T(8,128)}, f32[16,64,128]{2,1,0:T(8,128)S(1)}, u32[]{:S(2)}, u32[]{:S(2)}) collective-permute-start(f32[16,64,128]{2,1,0:T(8,128)} %mid.5), channel_id=1, source_target_pairs={{32,0},{0,32},{96,64},{64,96},{33,1},{1,33},{97,65},{65,97},{34,2}... | collective-permute-start | bytes 1572872 | tf_op jit(solution)/shard_map/ppermute | solution.py:556
  6.7 0.8 slice_select_fusion
  7.5 0.7 collective-permute-start.2
  8.2 0.9 fusion.3
  9.1 1.0 %fusion.1 = (f32[16,16,128]{2,1,0:T(8,128)S(1)}, f32[16,16,128]{2,1,0:T(8,128)S(1)}) fusion(f32[16,64,128]{2,1,0:T(8,128)} %mid.5), kind=kLoop, calls=%fused_computation.23 | loop fusion | bytes 524288 | tf_op jit(solution)/shard_map/slice | solution.py:618
  10.3 8.7 %collective-permute-done.3 = f32[1,64,128]{2,1,0:T(8,128)S(1)} collective-permute-done((f32[1,64,128]{2,1,0:T(8,128)S(1)}, f32[1,64,128]{2,1,0:T(8,128)S(1)}, u32[]{:S(2)}, u32[]{:S(2)}) %collective-permute-start.3) | collective-permute-done | bytes 32800 | tf_op jit(solution)/shard_map/ppermute | solution.py:556
  19.3 1.6 %collective-permute-start.5 = (f32[49,16,128]{2,1,0:T(8,128)S(1)}, f32[49,16,128]{2,1,0:T(8,128)S(1)}, u32[]{:S(2)}, u32[]{:S(2)}) collective-permute-start(f32[49,16,128]{2,1,0:T(8,128)S(1)} %broadcast_select_fusion.4), channel_id=1, source_target_pairs={{0,4},{4,0},{8,12},{12,8},{16,20},{20,16},{24,28},{28,24},{1,5},{5... | collective-permute-start | bytes 1204232 | tf_op jit(solution)/shard_map/ppermute | solution.py:584
  20.9 3.1 %collective-permute-start.4 = (f32[49,16,128]{2,1,0:T(8,128)S(1)}, f32[49,16,128]{2,1,0:T(8,128)S(1)}, u32[]{:S(2)}, u32[]{:S(2)}) collective-permute-start(f32[49,16,128]{2,1,0:T(8,128)S(1)} %get-tuple-element.45), channel_id=1, source_target_pairs={{4,8},{12,16},{20,24},{8,4},{16,12},{24,20},{5,9},{13,17},{21,25},... | collective-permute-start | bytes 1204232 | tf_op jit(solution)/shard_map/ppermute | solution.py:583
  24.1 6.1 %collective-permute-done.4 = f32[49,16,128]{2,1,0:T(8,128)S(1)} collective-permute-done((f32[49,16,128]{2,1,0:T(8,128)S(1)}, f32[49,16,128]{2,1,0:T(8,128)S(1)}, u32[]{:S(2)}, u32[]{:S(2)}) %collective-permute-start.4) | collective-permute-done | bytes 401440 | tf_op jit(solution)/shard_map/ppermute | solution.py:583
  30.3 0.9 strips.1
  31.2 1.5 %collective-permute-start.7 = (f32[584,128]{1,0:T(8,128)S(1)}, f32[584,128]{1,0:T(8,128)S(1)}, u32[]{:S(2)}, u32[]{:S(2)}) collective-permute-start(f32[584,128]{1,0:T(8,128)S(1)} %get-tuple-element.32), channel_id=1, source_target_pairs={{1,0},{0,1},{3,2},{2,3},{5,4},{4,5},{7,6},{6,7},{9,8},{8,9},{11,10... | collective-permute-start | bytes 897032 | tf_op jit(solution)/shard_map/ppermute | solution.py:556
  32.7 0.7 collective-permute-start.6
  33.4 3.7 %inner.1.inside = f32[16,64,128]{2,1,0:T(8,128)S(1)} custom-call(s32[96]{0:T(128)S(1)} %reshape.8.summed, f32[16,64,128]{2,1,0:T(8,128)S(1)} %copy-done, f32[16,64,128]{2,1,0:T(8,128)S(1)} %get-tuple-element.27.zlo, f32[16,64,128]{2,1,0:T(8,128)S(1)} %get-tuple-element.26.zhi, f32[49,16,128]{2,1,0:T(8,128)S(1)} %get-tuple-element.29.ylo, ...), custom_call_target="tpu_custom_call" | custom-call | tf_op jit(solution)/shard_map/inner/pallas_call | solution.py:186
  37.2 0.8 copy-done.2
  38.0 5.3 %terms.1 = f32[32,128]{1,0:T(8,128)S(1)} custom-call(s32[96]{0:T(128)S(1)} %reshape.8.summed, f32[16,64,128]{2,1,0:T(8,128)S(1)} %copy-done.1, f32[1,64,128]{2,1,0:T(8,128)S(1)} %get-tuple-element.15.rzlo, f32[1,64,128]{2,1,0:T(8,128)S(1)} %get-tuple-element.16.rzhi, f32[16,64,128]{2,1,0:T(8,128)S(1)} %copy-done, f32[16,64,128]{2,1,0:T(8,128)S(1)} %get-tuple-element.27.zlo, ...), custom_call_target="tpu_custom_call" | custom-call | tf_op jit(solution)/shard_map/terms/pallas_call | solution.py:307
  43.3 0.8 collective-permute-start.10
  44.1 2.5 %collective-permute-start.9 = (f32[32,128]{1,0:T(8,128)S(1)}, f32[32,128]{1,0:T(8,128)S(1)}, u32[]{:S(2)}, u32[]{:S(2)}) collective-permute-start(f32[32,128]{1,0:T(8,128)S(1)} %terms.1), channel_id=1, source_target_pairs={{64,0},{96,32},{0,64},{32,96},{65,1},{97,33},{1,65},{33,97},{66,2}... | collective-permute-start | bytes 49160 | tf_op jit(solution)/shard_map/ppermute | solution.py:556
  46.6 0.5 collective-permute-done.10
  47.2 1.0 %collective-permute-done.9 = f32[32,128]{1,0:T(8,128)S(1)} collective-permute-done((f32[32,128]{1,0:T(8,128)S(1)}, f32[32,128]{1,0:T(8,128)S(1)}, u32[]{:S(2)}, u32[]{:S(2)}) %collective-permute-start.9) | collective-permute-done | bytes 16416 | tf_op jit(solution)/shard_map/ppermute | solution.py:556
  48.2 1.0 %collective-permute-done.8 = f32[32,128]{1,0:T(8,128)S(1)} collective-permute-done((f32[32,128]{1,0:T(8,128)S(1)}, f32[32,128]{1,0:T(8,128)S(1)}, u32[]{:S(2)}, u32[]{:S(2)}) %collective-permute-start.8) | collective-permute-done | bytes 16416 | tf_op jit(solution)/shard_map/ppermute | solution.py:556
  49.3 4.6 %collective-permute-start.11 = (f32[112,128]{1,0:T(8,128)S(1)}, f32[112,128]{1,0:T(8,128)S(1)}, u32[]{:S(2)}, u32[]{:S(2)}) collective-permute-start(f32[112,128]{1,0:T(8,128)S(1)} %concatenate.27), channel_id=1, source_target_pairs={{2,0},{3,1},{0,2},{1,3},{6,4},{7,5},{4,6},{5,7},{10,8},{11,9},{8,1... | collective-permute-start | bytes 172040 | tf_op jit(solution)/shard_map/ppermute | solution.py:556
  53.9 1.6 %collective-permute-done.11 = f32[112,128]{1,0:T(8,128)S(1)} collective-permute-done((f32[112,128]{1,0:T(8,128)S(1)}, f32[112,128]{1,0:T(8,128)S(1)}, u32[]{:S(2)}, u32[]{:S(2)}) %collective-permute-start.11) | collective-permute-done | bytes 57376 | tf_op jit(solution)/shard_map/ppermute | solution.py:556
  55.6 6.0 %collective-permute-start.13 = (f32[224,128]{1,0:T(8,128)S(1)}, f32[224,128]{1,0:T(8,128)S(1)}, u32[]{:S(2)}, u32[]{:S(2)}) collective-permute-start(f32[224,128]{1,0:T(8,128)S(1)} %concatenate.28), channel_id=1, source_target_pairs={{16,0},{20,4},{24,8},{28,12},{0,16},{4,20},{8,24},{12,28},{17,1},{... | collective-permute-start | bytes 344072 | tf_op jit(solution)/shard_map/ppermute | solution.py:556
  61.6 2.2 %collective-permute-done.13 = f32[224,128]{1,0:T(8,128)S(1)} collective-permute-done((f32[224,128]{1,0:T(8,128)S(1)}, f32[224,128]{1,0:T(8,128)S(1)}, u32[]{:S(2)}, u32[]{:S(2)}) %collective-permute-start.13) | collective-permute-done | bytes 114720 | tf_op jit(solution)/shard_map/ppermute | solution.py:556
  63.8 1.1 %collective-permute-start.16 = (f32[448,128]{1,0:T(8,128)S(1)}, f32[448,128]{1,0:T(8,128)S(1)}, u32[]{:S(2)}, u32[]{:S(2)}) collective-permute-start(f32[448,128]{1,0:T(8,128)S(1)} %pad_maximum_fusion.2), channel_id=1, source_target_pairs={{3,0},{2,1},{1,2},{0,3},{7,4},{6,5},{5,6},{4,7},{11,8},{10,9},{9,1... | collective-permute-start | bytes 688136 | tf_op jit(solution)/shard_map/ppermute | solution.py:556
  64.9 0.4 collective-permute-done.12
  65.3 1.6 %collective-permute-start.15 = (f32[448,128]{1,0:T(8,128)S(1)}, f32[448,128]{1,0:T(8,128)S(1)}, u32[]{:S(2)}, u32[]{:S(2)}) collective-permute-start(f32[448,128]{1,0:T(8,128)S(1)} %concatenate.29), channel_id=1, source_target_pairs={{1,0},{0,1},{3,2},{2,3},{5,4},{4,5},{7,6},{6,7},{9,8},{8,9},{11,10... | collective-permute-start | bytes 688136 | tf_op jit(solution)/shard_map/ppermute | solution.py:556
  66.9 3.1 %collective-permute-done.16 = f32[448,128]{1,0:T(8,128)S(1)} collective-permute-done((f32[448,128]{1,0:T(8,128)S(1)}, f32[448,128]{1,0:T(8,128)S(1)}, u32[]{:S(2)}, u32[]{:S(2)}) %collective-permute-start.16) | collective-permute-done | bytes 229408 | tf_op jit(solution)/shard_map/ppermute | solution.py:556
  70.4 6.3 %collective-permute-start.17 = (f32[1792,128]{1,0:T(8,128)S(1)}, f32[1792,128]{1,0:T(8,128)S(1)}, u32[]{:S(2)}, u32[]{:S(2)}) collective-permute-start(f32[1792,128]{1,0:T(8,128)S(1)} %concatenate.31.part0), channel_id=1, source_target_pairs={{4,0},{0,4},{12,8},{8,12},{20,16},{16,20},{28,24},{24,28},{5,1},{1... | collective-permute-start | bytes 2752520 | tf_op jit(solution)/shard_map/ppermute | solution.py:556
  76.8 2.0 %collective-permute-done.17.part1 = f32[1792,128]{1,0:T(8,128)S(1)} collective-permute-done((f32[1792,128]{1,0:T(8,128)S(1)}, f32[1792,128]{1,0:T(8,128)S(1)}, u32[]{:S(2)}, u32[]{:S(2)}) %collective-permute-start.17) | collective-permute-done | bytes 917536 | tf_op jit(solution)/shard_map/ppermute | solution.py:556
  78.8 14.6 %cg.1 = (f32[3,5,2,9]{3,2,1,0:T(2,128)}, f32[3,5,2,9]{3,2,1,0:T(2,128)}) custom-call(s32[3]{0:T(128)S(1)} %pad_add_fusion.where, f32[1792,128]{1,0:T(8,128)S(1)} %concatenate.31.part0, f32[1792,128]{1,0:T(8,128)S(1)} %collective-permute-done.17.part1), custom_call_target="tpu_custom_call" | custom-call | tf_op jit(solution)/shard_map/cg/pallas_call | solution.py:539
  (53 shorter events, 1.5 us)
Async XLA Ops:
  0.6 18.4 %collective-permute-start.1 = (f32[16,64,128]{2,1,0:T(8,128)}, f32[16,64,128]{2,1,0:T(8,128)S(1)}, u32[]{:S(2)}, u32[]{:S(2)}) collective-permute-start(f32[16,64,128]{2,1,0:T(8,128)} %mid.5), channel_id=1, source_target_pairs={{32,64},{64,32},{33,65},{65,33},{34,66},{66,34},{35,67},{67,35},{3... | collective-permute-start | bytes 1572872 | tf_op jit(solution)/shard_map/ppermute | solution.py:562
  1.3 17.7 %collective-permute-start = (f32[16,64,128]{2,1,0:T(8,128)}, f32[16,64,128]{2,1,0:T(8,128)S(1)}, u32[]{:S(2)}, u32[]{:S(2)}) collective-permute-start(f32[16,64,128]{2,1,0:T(8,128)} %mid.5), channel_id=1, source_target_pairs={{32,0},{0,32},{96,64},{64,96},{33,1},{1,33},{97,65},{65,97},{34,2}... | collective-permute-start | bytes 1572872 | tf_op jit(solution)/shard_map/ppermute | solution.py:556
  7.5 11.5 %collective-permute-start.3 = (f32[1,64,128]{2,1,0:T(8,128)S(1)}, f32[1,64,128]{2,1,0:T(8,128)S(1)}, u32[]{:S(2)}, u32[]{:S(2)}) collective-permute-start(f32[1,64,128]{2,1,0:T(8,128)S(1)} %get-tuple-element.42), channel_id=1, source_target_pairs={{32,0},{0,32},{96,64},{64,96},{33,1},{1,33},{97,65},{65,97},{34,2}... | collective-permute-start | bytes 98312 | tf_op jit(solution)/shard_map/ppermute | solution.py:556
  7.5 11.4 %collective-permute-start.2 = (f32[1,64,128]{2,1,0:T(8,128)S(1)}, f32[1,64,128]{2,1,0:T(8,128)S(1)}, u32[]{:S(2)}, u32[]{:S(2)}) collective-permute-start(f32[1,64,128]{2,1,0:T(8,128)S(1)} %get-tuple-element.43), channel_id=1, source_target_pairs={{32,64},{64,32},{33,65},{65,33},{34,66},{66,34},{35,67},{67,35},{3... | collective-permute-start | bytes 98312 | tf_op jit(solution)/shard_map/ppermute | solution.py:562
  9.1 1.0 %copy-start.6 = (s32[3,2,5,9]{3,1,2,0:T(2,128)S(1)}, s32[3,2,5,9]{3,1,2,0:T(2,128)}, u32[]{:S(2)}) copy-start(s32[3,2,5,9]{3,1,2,0:T(2,128)} %param.9) | copy-start | bytes 3244
  19.3 4.8 %collective-permute-start.5 = (f32[49,16,128]{2,1,0:T(8,128)S(1)}, f32[49,16,128]{2,1,0:T(8,128)S(1)}, u32[]{:S(2)}, u32[]{:S(2)}) collective-permute-start(f32[49,16,128]{2,1,0:T(8,128)S(1)} %broadcast_select_fusion.4), channel_id=1, source_target_pairs={{0,4},{4,0},{8,12},{12,8},{16,20},{20,16},{24,28},{28,24},{1,5},{5... | collective-permute-start | bytes 1204232 | tf_op jit(solution)/shard_map/ppermute | solution.py:584
  20.9 9.3 %collective-permute-start.4 = (f32[49,16,128]{2,1,0:T(8,128)S(1)}, f32[49,16,128]{2,1,0:T(8,128)S(1)}, u32[]{:S(2)}, u32[]{:S(2)}) collective-permute-start(f32[49,16,128]{2,1,0:T(8,128)S(1)} %get-tuple-element.45), channel_id=1, source_target_pairs={{4,8},{12,16},{20,24},{8,4},{16,12},{24,20},{5,9},{13,17},{21,25},... | collective-permute-start | bytes 1204232 | tf_op jit(solution)/shard_map/ppermute | solution.py:583
  24.1 6.2 %copy-start = (f32[16,64,128]{2,1,0:T(8,128)S(1)}, f32[16,64,128]{2,1,0:T(8,128)}, u32[]{:S(2)}) copy-start(f32[16,64,128]{2,1,0:T(8,128)} %mid.5) | copy-start | bytes 1572868
  24.1 6.2 %copy-start.1 = (f32[16,64,128]{2,1,0:T(8,128)S(1)}, f32[16,64,128]{2,1,0:T(8,128)}, u32[]{:S(2)}) copy-start(f32[16,64,128]{2,1,0:T(8,128)} %ref.3) | copy-start | bytes 1572868
  31.2 5.9 %collective-permute-start.7 = (f32[584,128]{1,0:T(8,128)S(1)}, f32[584,128]{1,0:T(8,128)S(1)}, u32[]{:S(2)}, u32[]{:S(2)}) collective-permute-start(f32[584,128]{1,0:T(8,128)S(1)} %get-tuple-element.32), channel_id=1, source_target_pairs={{1,0},{0,1},{3,2},{2,3},{5,4},{4,5},{7,6},{6,7},{9,8},{8,9},{11,10... | collective-permute-start | bytes 897032 | tf_op jit(solution)/shard_map/ppermute | solution.py:556
  32.7 4.4 %collective-permute-start.6 = (f32[584,128]{1,0:T(8,128)S(1)}, f32[584,128]{1,0:T(8,128)S(1)}, u32[]{:S(2)}, u32[]{:S(2)}) collective-permute-start(f32[584,128]{1,0:T(8,128)S(1)} %get-tuple-element.33), channel_id=1, source_target_pairs={{1,2},{2,1},{5,6},{6,5},{9,10},{10,9},{13,14},{14,13},{17,18},{18,... | collective-permute-start | bytes 897032 | tf_op jit(solution)/shard_map/ppermute | solution.py:562
  37.1 0.9 copy-start.2
  37.1 0.9 copy-start.3
  37.1 0.9 copy-start.4
  37.1 0.9 copy-start.5
  43.3 3.9 %collective-permute-start.10 = (f32[32,128]{1,0:T(8,128)S(1)}, f32[32,128]{1,0:T(8,128)S(1)}, u32[]{:S(2)}, u32[]{:S(2)}) collective-permute-start(f32[32,128]{1,0:T(8,128)S(1)} %terms.1), channel_id=1, source_target_pairs={{96,0},{64,32},{32,64},{0,96},{97,1},{65,33},{33,65},{1,97},{98,2}... | collective-permute-start | bytes 49160 | tf_op jit(solution)/shard_map/ppermute | solution.py:556
  44.1 4.1 %collective-permute-start.9 = (f32[32,128]{1,0:T(8,128)S(1)}, f32[32,128]{1,0:T(8,128)S(1)}, u32[]{:S(2)}, u32[]{:S(2)}) collective-permute-start(f32[32,128]{1,0:T(8,128)S(1)} %terms.1), channel_id=1, source_target_pairs={{64,0},{96,32},{0,64},{32,96},{65,1},{97,33},{1,65},{33,97},{66,2}... | collective-permute-start | bytes 49160 | tf_op jit(solution)/shard_map/ppermute | solution.py:556
  46.6 2.6 %collective-permute-start.8 = (f32[32,128]{1,0:T(8,128)S(1)}, f32[32,128]{1,0:T(8,128)S(1)}, u32[]{:S(2)}, u32[]{:S(2)}) collective-permute-start(f32[32,128]{1,0:T(8,128)S(1)} %terms.1), channel_id=1, source_target_pairs={{32,0},{0,32},{96,64},{64,96},{33,1},{1,33},{97,65},{65,97},{34,2}... | collective-permute-start | bytes 49160 | tf_op jit(solution)/shard_map/ppermute | solution.py:556
  49.3 6.2 %collective-permute-start.11 = (f32[112,128]{1,0:T(8,128)S(1)}, f32[112,128]{1,0:T(8,128)S(1)}, u32[]{:S(2)}, u32[]{:S(2)}) collective-permute-start(f32[112,128]{1,0:T(8,128)S(1)} %concatenate.27), channel_id=1, source_target_pairs={{2,0},{3,1},{0,2},{1,3},{6,4},{7,5},{4,6},{5,7},{10,8},{11,9},{8,1... | collective-permute-start | bytes 172040 | tf_op jit(solution)/shard_map/ppermute | solution.py:556
  55.5 6.1 %collective-permute-start.14 = (f32[224,128]{1,0:T(8,128)S(1)}, f32[224,128]{1,0:T(8,128)S(1)}, u32[]{:S(2)}, u32[]{:S(2)}) collective-permute-start(f32[224,128]{1,0:T(8,128)S(1)} %concatenate.28), channel_id=1, source_target_pairs={{24,0},{28,4},{16,8},{20,12},{8,16},{12,20},{0,24},{4,28},{25,1},{... | collective-permute-start | bytes 344072 | tf_op jit(solution)/shard_map/ppermute | solution.py:556
  55.6 8.2 %collective-permute-start.13 = (f32[224,128]{1,0:T(8,128)S(1)}, f32[224,128]{1,0:T(8,128)S(1)}, u32[]{:S(2)}, u32[]{:S(2)}) collective-permute-start(f32[224,128]{1,0:T(8,128)S(1)} %concatenate.28), channel_id=1, source_target_pairs={{16,0},{20,4},{24,8},{28,12},{0,16},{4,20},{8,24},{12,28},{17,1},{... | collective-permute-start | bytes 344072 | tf_op jit(solution)/shard_map/ppermute | solution.py:556
  61.6 3.7 %collective-permute-start.12 = (f32[224,128]{1,0:T(8,128)S(1)}, f32[224,128]{1,0:T(8,128)S(1)}, u32[]{:S(2)}, u32[]{:S(2)}) collective-permute-start(f32[224,128]{1,0:T(8,128)S(1)} %concatenate.28), channel_id=1, source_target_pairs={{8,0},{12,4},{0,8},{4,12},{24,16},{28,20},{16,24},{20,28},{9,1},{1... | collective-permute-start | bytes 344072 | tf_op jit(solution)/shard_map/ppermute | solution.py:556
  63.8 6.2 %collective-permute-start.16 = (f32[448,128]{1,0:T(8,128)S(1)}, f32[448,128]{1,0:T(8,128)S(1)}, u32[]{:S(2)}, u32[]{:S(2)}) collective-permute-start(f32[448,128]{1,0:T(8,128)S(1)} %pad_maximum_fusion.2), channel_id=1, source_target_pairs={{3,0},{2,1},{1,2},{0,3},{7,4},{6,5},{5,6},{4,7},{11,8},{10,9},{9,1... | collective-permute-start | bytes 688136 | tf_op jit(solution)/shard_map/ppermute | solution.py:556
  65.3 5.0 %collective-permute-start.15 = (f32[448,128]{1,0:T(8,128)S(1)}, f32[448,128]{1,0:T(8,128)S(1)}, u32[]{:S(2)}, u32[]{:S(2)}) collective-permute-start(f32[448,128]{1,0:T(8,128)S(1)} %concatenate.29), channel_id=1, source_target_pairs={{1,0},{0,1},{3,2},{2,3},{5,4},{4,5},{7,6},{6,7},{9,8},{8,9},{11,10... | collective-permute-start | bytes 688136 | tf_op jit(solution)/shard_map/ppermute | solution.py:556
  70.4 8.4 %collective-permute-start.17 = (f32[1792,128]{1,0:T(8,128)S(1)}, f32[1792,128]{1,0:T(8,128)S(1)}, u32[]{:S(2)}, u32[]{:S(2)}) collective-permute-start(f32[1792,128]{1,0:T(8,128)S(1)} %concatenate.31.part0), channel_id=1, source_target_pairs={{4,0},{0,4},{12,8},{8,12},{20,16},{16,20},{28,24},{24,28},{5,1},{1... | collective-permute-start | bytes 2752520 | tf_op jit(solution)/shard_map/ppermute | solution.py:556
